TPU v7x, 128 devices: a whole 4x4x4 slice. The times are simulated.
128 devices in a mesh: store: 16 (over x, y), ctx: 8 (over z, core).
Axes of the slice: x: 4, y: 4, z: 4, core: 2. Of those that a mesh axis runs over, the one named last changes fastest.
Arguments:
- tokens: bfloat16 [2048, 8192], P('store'), may hold values from -6 to 6
- joined_weight: bfloat16 [8192, 8, 1280], P(None, 'ctx'), may hold values from -0.0625 to 0.0625
- down_weight: bfloat16 [128, 8192, 64], P('store', 'ctx'), may hold values from -0.0625 to 0.0625
- up_weight: bfloat16 [128, 64, 8, 1280], P('store', None, 'ctx'), may hold values from -0.75 to 0.75
- adapter_per_request: int32 [2048], replicated, may hold values from 0 to 127, as said below
- adapter_store_slot: int32 [128], replicated, may hold values from 0 to 127, as said below
- prefix_block_list: int32 [2048, 8], P('store'), may hold values from 0 to 255, as said below
- prefix_length: int32 [2048], P('store'), may hold values from 1 to 128, as said below
- key_value_pool: bfloat16 [4096, 8, 256], P(('store', 'ctx')), may hold values from -400 to 400
Outputs:
- attn: bfloat16 [2048, 8, 1024], P('store', 'ctx')
Inputs may be any that keep to these rules, and one draw needn't show every extreme that they name: `adapter_store_slot`: A permutation; slot s belongs to owner s // 8, which holds slots in store order. `adapter_per_request`: among the 128 requests of one store shard, at most 16 use adapters of one owner; on every shard one owner, the same for all shards, receives exactly 16. `prefix_block_list`: the 8 blocks of a request are distinct and lie in its store shard's range of 16 blocks, rows i * 128 to (i+1) * 128 - 1 using blocks i * 16 to (i+1) * 16 - 1. `prefix_length`: every store shard has a request of length 128.
All inputs are finite; a program needn't handle non-finite values.
Results may differ from a plain program's by a relative error of at most 0.02.
The roundings to bfloat16 on the way count: a program that leaves them out, or rounds other values in their place, can miss the bound.
Values may be sent and summed in bfloat16 or wider, within the bound.
No kernel may reach another device: no remote copies, remote signals or barrier semaphores. Data moves between devices by JAX's collectives and lax.ppermute only.
A program may use at most 128 MiB of HBM per device.

v0:
```python
import jax
import jax.numpy as jnp
from jax import lax
from jax.sharding import PartitionSpec as P

QUERY_PER_KEY = 8
HEAD_SIZE = 128
CAP = 16
BLK = 16
ROPE_THETA = 500000.0
ADAPTER_SCALE = 2.0


def rotary_apply(vec, token_position):
    half = vec.shape[-1] // 2
    freq = jnp.power(ROPE_THETA, -(jnp.arange(half, dtype=jnp.float32) * 2.0 / vec.shape[-1]))
    angle = token_position[..., None] * freq
    cosine = jnp.cos(angle)
    sine = jnp.sin(angle)
    initial_part = vec[..., :half]
    second = vec[..., half:]
    return jnp.concatenate(
        [initial_part * cosine - second * sine, initial_part * sine + second * cosine], axis=-1
    )


def prefix_mask(local_ids, lens, group_blocks, blk):
    listed = local_ids.shape[1]
    equal = local_ids[:, :, None] == jnp.arange(group_blocks, dtype=jnp.int32)[None, None, :]
    start = jnp.sum(
        jnp.where(equal, (jnp.arange(listed, dtype=jnp.int32) * blk)[None, :, None], 0), axis=1
    )
    present = jnp.any(equal, axis=1)
    offset = jnp.arange(blk, dtype=jnp.int32)
    live = present[:, :, None] & (start[:, :, None] + offset[None, None, :] < lens[:, None, None])
    return live.reshape(local_ids.shape[0], group_blocks * blk)


def attend(query_rows, key_new, value_new, keys, value_rows, live):
    scale = 1.0 / HEAD_SIZE**0.5
    pool_scores = (
        jnp.einsum("rhgd,thd->rhgt", query_rows, keys, preferred_element_type=jnp.float32) * scale
    )
    own = (
        jnp.einsum("rhgd,rhd->rhg", query_rows, key_new, preferred_element_type=jnp.float32) * scale
    )
    mask = live[:, None, None, :]
    pool_scores = jnp.where(mask, pool_scores, -jnp.inf)
    top = jnp.maximum(jnp.max(pool_scores, axis=-1), own)
    prob = jnp.where(mask, jnp.exp(pool_scores - top[..., None]), 0.0)
    prob_own = jnp.exp(own - top)
    total = jnp.sum(prob, axis=-1) + prob_own
    prob_low = prob.astype(jnp.bfloat16)
    own_low = prob_own.astype(jnp.bfloat16)
    mixed = jnp.einsum("rhgt,thd->rhgd", prob_low, value_rows, preferred_element_type=jnp.float32)
    mixed = (
        mixed
        + own_low.astype(jnp.float32)[..., None] * value_new.astype(jnp.float32)[:, :, None, :]
    )
    mixed = mixed / total[..., None]
    return mixed.astype(jnp.bfloat16).reshape(query_rows.shape[0], query_rows.shape[1], -1)


def routing(adapter_per_request, adapter_store_slot, shards, request_shard, shard_adapters):
    adapters = adapter_store_slot.shape[0]
    match = adapter_per_request[:, None] == jnp.arange(adapters, dtype=jnp.int32)[None, :]
    store_slot = jnp.sum(jnp.where(match, adapter_store_slot[None, :], 0), axis=1).reshape(
        shards, request_shard
    )
    owner = store_slot // shard_adapters
    owner_hot = (owner[:, :, None] == jnp.arange(shards, dtype=jnp.int32)[None, None, :]).astype(
        jnp.int32
    )
    counted = jnp.cumsum(owner_hot, axis=1) - 1
    rank = jnp.sum(owner_hot * counted, axis=2)
    return (store_slot, owner, rank)


def body(
    tokens,
    joined_weight,
    down_weight,
    up_weight,
    adapter_per_request,
    adapter_store_slot,
    prefix_block_list,
    prefix_length,
    key_value_pool,
):
    n_store = lax.axis_size("store")
    n_ctx = lax.axis_size("ctx")
    shard = lax.axis_index("store")
    member = lax.axis_index("ctx")
    request_shard = tokens.shape[0]
    d_model = tokens.shape[1]
    shard_adapters = down_weight.shape[0]
    width_slice = down_weight.shape[1]
    head_slice = joined_weight.shape[1]
    column_list = joined_weight.shape[2]
    whole_group = lax.all_gather(key_value_pool, "ctx", axis=0, tiled=True)
    group = lax.dynamic_slice_in_dim(whole_group, member * head_slice, head_slice, 1)
    store_slot, owner, rank = routing(
        adapter_per_request, adapter_store_slot, n_store, request_shard, shard_adapters
    )
    owner_mine = lax.dynamic_index_in_dim(owner, shard, 0, keepdims=False)
    rank_mine = lax.dynamic_index_in_dim(rank, shard, 0, keepdims=False)
    dest = owner_mine * CAP + rank_mine
    x_local = lax.dynamic_slice_in_dim(tokens, member * width_slice, width_slice, 1)
    outgoing = jnp.zeros((n_store * CAP, width_slice), jnp.bfloat16).at[dest].set(x_local)
    received_parts = lax.all_to_all(
        outgoing.reshape(n_store, CAP, width_slice),
        "store",
        split_axis=0,
        concat_axis=0,
        tiled=True,
    )
    local_slot = store_slot % shard_adapters
    selected = (owner == shard)[:, :, None] & (
        rank[:, :, None] == jnp.arange(CAP, dtype=jnp.int32)[None, None, :]
    )
    adapter_hot = selected[:, :, :, None] & (
        local_slot[:, :, None, None]
        == jnp.arange(shard_adapters, dtype=jnp.int32)[None, None, None, :]
    )
    adapter_hot = jnp.any(adapter_hot, axis=1)
    value_partial = jnp.einsum(
        "hbm,gmq->hbgq", received_parts, down_weight, preferred_element_type=jnp.float32
    )
    shrunk_part = jnp.sum(jnp.where(adapter_hot[..., None], value_partial, 0.0), axis=2)
    shrunk = lax.psum(shrunk_part, "ctx").astype(jnp.bfloat16)
    spread_rows = jnp.where(
        adapter_hot[..., None], shrunk[:, :, None, :], jnp.zeros((), jnp.bfloat16)
    )
    adapter_update = jnp.einsum(
        "oxbl,blpj->oxpj", spread_rows, up_weight, preferred_element_type=jnp.float32
    ).astype(jnp.bfloat16)
    returned = lax.all_to_all(adapter_update, "store", split_axis=0, concat_axis=0, tiled=True)
    update_mine = returned.reshape(n_store * CAP, head_slice, column_list)[dest]
    plain_projection = jnp.dot(
        tokens,
        joined_weight.reshape(d_model, head_slice * column_list),
        preferred_element_type=jnp.float32,
    )
    joined_projection = plain_projection.reshape(
        request_shard, head_slice, column_list
    ) + ADAPTER_SCALE * update_mine.astype(jnp.float32)
    token_position = prefix_length.astype(jnp.float32)
    query_rows = rotary_apply(
        joined_projection[:, :, : QUERY_PER_KEY * HEAD_SIZE].reshape(
            request_shard, head_slice, QUERY_PER_KEY, HEAD_SIZE
        ),
        token_position[:, None, None],
    ).astype(jnp.bfloat16)
    key_new = rotary_apply(
        joined_projection[:, :, QUERY_PER_KEY * HEAD_SIZE : (QUERY_PER_KEY + 1) * HEAD_SIZE],
        token_position[:, None],
    ).astype(jnp.bfloat16)
    value_new = joined_projection[:, :, (QUERY_PER_KEY + 1) * HEAD_SIZE :].astype(jnp.bfloat16)
    group_blocks = key_value_pool.shape[0] * n_ctx // BLK
    live = prefix_mask(prefix_block_list - shard * group_blocks, prefix_length, group_blocks, BLK)
    return attend(
        query_rows, key_new, value_new, group[:, :, :HEAD_SIZE], group[:, :, HEAD_SIZE:], live
    )


def solution(mesh):
    in_specs = (
        P("store", None),
        P(None, "ctx", None),
        P("store", "ctx", None),
        P("store", None, "ctx", None),
        P(),
        P(),
        P("store", None),
        P("store"),
        P(("store", "ctx"), None, None),
    )
    out_specs = P("store", "ctx", None)
    return jax.shard_map(body, mesh=mesh, in_specs=in_specs, out_specs=out_specs, check_vma=False)
```

profile of v0, /device:TPU:0, one launch (start us, length us, event | category | flops | bytes accessed | tf_op | source)
XLA Modules:
  0.0 103.6 jit_solution(7977212411898777867)
XLA Ops:
  6.5 1.7 %copy.72 = bf16[32,8,256]{2,0,1:T(8,128)(2,1)} copy(bf16[32,8,256]{2,1,0:T(8,128)(2,1)} %param.17) | data formatting | bytes 262144 | tf_op args[8]
  8.3 1.3 %select_reduce_fusion.1 = s32[2048]{0:T(1024)S(1)} fusion(s32[128]{0:T(128)} %param.14, s32[2048]{0:T(1024)} %param.13), kind=kLoop, calls=%fused_computation.25 | loop fusion | flops 784384 | bytes 16896 | tf_op jit(solution)/shard_map/reduce_sum | solution.py:67
  9.7 0.1 copy.73
  9.8 2.8 %select_reduce_fusion = s32[16,128]{0,1:T(8,128)S(1)} fusion(s32[16,128]{0,1:T(8,128)S(1)} %copy.73), kind=kOutput, calls=%fused_computation.21 | output fusion | flops 4356096 | bytes 16384 | tf_op jit(solution)/shard_map/jit(cumsum)/reduce_window_sum | solution.py:74
  12.7 2.0 %scatter_custom_fusion = bf16[256,1024]{1,0:T(8,128)(2,1)} fusion(s32[128]{0:T(128)S(1)} %fusion.66, bf16[128,8192]{1,0:T(8,128)(2,1)S(1)} %copy-done, s32[]{:T(128)} %constant.35.clone.1, s32[]{:T(128)S(6)} %select_n.75, bf16[]{:T(256)} %constant.73.clone.1), kind=kCustom, calls=%fused_computation.46 | custom fusion | bytes 786442 | tf_op jit(solution)/shard_map/scatter | solution.py:109
  14.6 7.1 %all-to-all-start = ((bf16[16,16,1024]{2,1,0:T(8,128)(2,1)}), bf16[16,16,1024]{2,1,0:T(8,128)(2,1)S(1)}, u32[]{:S(2)}, u32[]{:S(2)}) async-start(bf16[16,16,1024]{2,1,0:T(8,128)(2,1)} %bitcast.10), calls=%async_computation | async-start | bytes 1048576 | tf_op jit(solution)/shard_map/all_to_all | solution.py:110
  21.9 4.4 %and_reduce_fusion = pred[16,16,8]{2,1,0:T(8,128)(4,1)S(1)} fusion(pred[16,128,8]{1,2,0:T(8,128)(4,1)S(1)} %iota_compare_fusion.4, pred[16,128,16]{1,2,0:T(8,128)(4,1)S(1)} %fusion.41), kind=kLoop, calls=%fused_computation.27 | loop fusion | flops 522240 | bytes 51200 | tf_op jit(solution)/shard_map/reduce_or | solution.py:125
  26.3 0.1 copy.75
  26.5 6.8 %all-to-all-done = bf16[16,16,1024]{2,1,0:T(8,128)(2,1)S(1)} async-done(((bf16[16,16,1024]{2,1,0:T(8,128)(2,1)}), bf16[16,16,1024]{2,1,0:T(8,128)(2,1)S(1)}, u32[]{:S(2)}, u32[]{:S(2)}) %all-to-all-start) | async-done | bytes 524320 | tf_op jit(solution)/shard_map/all_to_all | solution.py:110
  33.3 2.0 %fusion.12 = f32[16,16,64]{2,1,0:T(8,128)S(1)} fusion(bf16[8,1024,64]{1,2,0:T(8,128)(2,1)} %param.11, bf16[16,16,1024]{2,1,0:T(8,128)(2,1)S(1)} %all-to-all-done, pred[16,16,8]{1,2,0:T(8,128)(4,1)S(1)} %copy.75), kind=kOutput, calls=%fused_computation.13 | convolution fusion | flops 268681216 | bytes 1640448 | tf_op jit(solution)/shard_map/hbm,gmq->hbgq/dot_general | solution.py:126
  35.3 26.7 %psum.7 = bf16[16,16,64]{2,1,0:T(8,128)(2,1)S(1)} all-reduce(f32[16,16,64]{2,1,0:T(8,128)S(1)} %fusion.12), channel_id=1, replica_groups=mesh['store'=16,'ctx'=8] {'ctx'}, use_global_device_ids=true, to_apply=%region_8.9 | all-reduce | flops 16384 | bytes 98304 | tf_op jit(solution)/shard_map/psum | solution.py:130
  62.0 3.0 %fusion.6 = bf16[16,16,1,1280]{3,1,2,0:T(8,128)(2,1)} fusion(bf16[8,64,1,1280]{3,1,2,0:T(8,128)(2,1)} %param.12, pred[16,16,8]{1,2,0:T(8,128)(4,1)S(1)} %copy.75, bf16[16,16,64]{2,1,0:T(8,128)(2,1)S(1)} %psum.7), kind=kOutput, calls=%fused_computation.7 | convolution fusion | flops 336003072 | bytes 2000896 | tf_op jit(solution)/shard_map/oxbl,blpj->oxpj/dot_general | solution.py:134
  65.0 3.8 %all-to-all-start.1 = ((bf16[16,16,1,1280]{3,1,2,0:T(8,128)(2,1)}), bf16[16,16,1,1280]{3,1,2,0:T(8,128)(2,1)S(1)}, u32[]{:S(2)}, u32[]{:S(2)}) async-start(bf16[16,16,1,1280]{3,1,2,0:T(8,128)(2,1)} %fusion.6), calls=%async_computation.1 | async-start | bytes 1310720 | tf_op jit(solution)/shard_map/all_to_all | solution.py:137
  68.8 0.1 add.102
  68.9 0.1 select_reduce_fusion.2
  69.0 0.1 fusion.42
  69.1 0.3 multiply_cosine_fusion.1
  69.4 10.1 %all-to-all-done.1 = bf16[16,16,1,1280]{3,1,2,0:T(8,128)(2,1)S(1)} async-done(((bf16[16,16,1,1280]{3,1,2,0:T(8,128)(2,1)}), bf16[16,16,1,1280]{3,1,2,0:T(8,128)(2,1)S(1)}, u32[]{:S(2)}, u32[]{:S(2)}) %all-to-all-start.1) | async-done | bytes 655392 | tf_op jit(solution)/shard_map/all_to_all | solution.py:137
  79.5 1.6 %gather_fusion = bf16[128,1280]{1,0:T(8,128)(2,1)} fusion(bf16[256,1280]{1,0:T(8,128)(2,1)S(1)} %bitcast.144, s32[1024]{0:T(1024)S(1)} %pad_clamp_fusion), kind=kCustom, calls=%fused_computation | custom fusion | bytes 655872 | tf_op jit(solution)/shard_map/gather | solution.py:138
  81.2 9.9 %fusion.7 = f32[128,1,1280]{2,0,1:T(8,128)S(1)} fusion(bf16[128,8192]{1,0:T(8,128)(2,1)S(1)} %copy-done, bf16[8192,1,1280]{2,0,1:T(8,128)(2,1)} %param.10, bf16[128,1280]{1,0:T(8,128)(2,1)} %gather_fusion), kind=kOutput, calls=%fused_computation.8 | convolution fusion | flops 2684846080 | bytes 24051712 | tf_op jit(solution)/shard_map/dot_general | solution.py:139
  91.1 0.1 copy.94
  91.2 0.7 copy.82
  91.9 0.3 fusion.56
  92.3 0.1 maximum_bitcast_fusion
  92.3 0.2 fusion.69
  92.5 0.2 fusion.31
  92.8 0.1 pad_maximum_fusion
  92.9 0.3 fusion.38
  93.3 1.2 %fusion.70 = (f32[128,8]{0,1:T(8,128)S(1)}, f32[128,1,8,256]{0,3,2,1:T(8,128)S(1)}) fusion(bf16[128,8,128]{2,0,1:T(8,128)(2,1)S(1)} %pad_maximum_fusion, bf16[256,8,256]{2,0,1:T(8,128)(2,1)} %all-gather.2.cloned.1.call-done, s32[]{:T(128)S(6)} %select_n.68, pred[128,256]{0,1:T(8,128)(4,1)S(1)} %fusion.42), kind=kOutput, calls=%fused_computation.112 | convolution fusion | flops 67894272 | bytes 1413124 | tf_op jit(solution)/shard_map/rhgd,thd->rhgt/dot_general | solution.py:42
  94.5 0.2 fusion.20
  94.7 1.2 %fusion.16 = bf16[128,1,8,128]{0,3,2,1:T(8,128)(2,1)S(1)} fusion(f32[128,1,8,256]{0,3,2,1:T(8,128)S(1)} %get-tuple-element.18, f32[128,8]{0,1:T(8,128)S(1)} %fusion.60, pred[128,256]{0,1:T(8,128)(4,1)S(1)} %fusion.42, f32[128,8]{0,1:T(8,128)S(1)} %get-tuple-element.12, f32[128,128]{0,1:T(8,128)S(1)} %copy-done.1, f32[128,8]{0,1:T(8,128)S(1)} %get-tuple-element.11, ...), kind=kOutput, calls=%fused_computation.18 | convolution fusion | flops 68419584 | bytes 1486856 | tf_op jit(solution)/shard_map/rhgt,thd->rhgd/dot_general | solution.py:55
  95.9 0.9 copy.83
  (29 shorter events, 0.4 us)
Async XLA Ops:
  6.5 6.1 %copy-start = (bf16[128,8192]{1,0:T(8,128)(2,1)S(1)}, bf16[128,8192]{1,0:T(8,128)(2,1)}, u32[]{:S(2)}) copy-start(bf16[128,8192]{1,0:T(8,128)(2,1)} %param.9) | copy-start | bytes 6291460
  6.5 19.9 %copy-start.2 = (s32[128,8]{0,1:T(8,128)S(1)}, s32[128,8]{0,1:T(8,128)}, u32[]{:S(2)}) copy-start(s32[128,8]{0,1:T(8,128)} %param.15) | copy-start | bytes 12292
  6.5 86.7 %all-gather.2.cloned.1.call-start = ((), (), s32[]{:S(2)}) async-start(), calls=%async_computation.2 | async-start | bytes 1179648 | tf_op jit(solution)/shard_map/all_gather | solution.py:100
  14.6 18.6 %all-to-all-start = ((bf16[16,16,1024]{2,1,0:T(8,128)(2,1)}), bf16[16,16,1024]{2,1,0:T(8,128)(2,1)S(1)}, u32[]{:S(2)}, u32[]{:S(2)}) async-start(bf16[16,16,1024]{2,1,0:T(8,128)(2,1)} %bitcast.10), calls=%async_computation | async-start | bytes 1048576 | tf_op jit(solution)/shard_map/all_to_all | solution.py:110
  62.0 6.8 %copy-start.3 = (s32[128]{0:T(128)S(1)}, s32[128]{0:T(128)}, u32[]{:S(2)}) copy-start(s32[128]{0:T(128)} %param.16) | copy-start | bytes 1540
  65.0 14.6 %all-to-all-start.1 = ((bf16[16,16,1,1280]{3,1,2,0:T(8,128)(2,1)}), bf16[16,16,1,1280]{3,1,2,0:T(8,128)(2,1)S(1)}, u32[]{:S(2)}, u32[]{:S(2)}) async-start(bf16[16,16,1,1280]{3,1,2,0:T(8,128)(2,1)} %fusion.6), calls=%async_computation.1 | async-start | bytes 1310720 | tf_op jit(solution)/shard_map/all_to_all | solution.py:137
  92.8 1.9 %copy-start.1 = (f32[128,128]{0,1:T(8,128)S(1)}, f32[128,128]{0,1:T(8,128)}, u32[]{:S(2)}) copy-start(f32[128,128]{0,1:T(8,128)} %copy.82) | copy-start | bytes 196612
Sparse Core Ops, SparseCore 0:
  9.1 26.0 all-gather.1
where the time goes:
time: 104 us
  blocking collectives  26.7 us (26%)
  matrix products  17.5 us (17%)
  waiting for transfers between devices  16.9 us (16%)
  between operations  13.7 us (13%)
  starting transfers between devices  10.9 us (10%)
  other arithmetic  10.2 us (10%)
  local copies, waits for them, and re-layouts  7.7 us (7%)
    psum x1, blocking collectives, body(): shrunk = lax.psum(shrunk_part, 'ctx').astype(jnp.bfloat16)  26.7 us
    all_to_all x1, waiting for transfers between devices, body(): lax.all_to_all(adapter_update, 'store', split_axis=0, concat_axis=0, tile...  10.1 us
    dot_general x1, matrix products, body(): jnp.dot(tokens, joined_weight.reshape(d_model, head_slice * column_list),...  9.86 us
    all_to_all x1, starting transfers between devices, body(): lax.all_to_all(outgoing.reshape(n_store, CAP, width_slice), 'store', spli...  7.12 us
    all_to_all x1, waiting for transfers between devices, body(): lax.all_to_all(outgoing.reshape(n_store, CAP, width_slice), 'store', spli...  6.79 us
    reduce_or x1, other arithmetic, body(): adapter_hot = jnp.any(adapter_hot, axis=1)  4.45 us
    all_to_all x1, starting transfers between devices, body(): lax.all_to_all(adapter_update, 'store', split_axis=0, concat_axis=0, tile...  3.81 us
    dot_general x1, matrix products, body(): jnp.einsum('oxbl,blpj->oxpj', spread_rows, up_weight, preferred_element_t...  2.99 us
  transfers between devices with their start and end apart: 3, of which 2 were waited for; matrix products, arithmetic and copies ran while one was open for 29% of the time, Pallas kernels for 0%

commit v1 on v0

--- a/solution.py
+++ b/solution.py
@@ -9,6 +9,12 @@
 BLK = 16
 ROPE_THETA = 500000.0
 ADAPTER_SCALE = 2.0
+
+
+def summed_here(array, axis):
+    parts = lax.all_gather(array, axis, axis=0, tiled=False)
+    total = parts.sum(axis=0)
+    return total
 
 
 def rotary_apply(vec, token_position):
@@ -127,7 +133,7 @@
         "hbm,gmq->hbgq", received_parts, down_weight, preferred_element_type=jnp.float32
     )
     shrunk_part = jnp.sum(jnp.where(adapter_hot[..., None], value_partial, 0.0), axis=2)
-    shrunk = lax.psum(shrunk_part, "ctx").astype(jnp.bfloat16)
+    shrunk = summed_here(shrunk_part, "ctx").astype(jnp.bfloat16)
     spread_rows = jnp.where(
         adapter_hot[..., None], shrunk[:, :, None, :], jnp.zeros((), jnp.bfloat16)
     )

time: 104 us -> 95.5 us (0.918)
  blocking collectives: 26.7 us -> 15.2 us
  waiting for transfers between devices: 16.9 us -> 19.7 us
    psum x1 -> x0, blocking collectives: 26.7 us -> none  [body(): shrunk = lax.psum(shrunk_part, 'ctx').astype(jnp.bfloat16)]
    all_gather x0 -> x1, blocking collectives: none -> 15.2 us  [summed_here(): parts = lax.all_gather(array, axis, axis=0, tiled=False)]
    all_to_all x1, waiting for transfers between devices: 10.1 us -> 12.9 us  [body(): lax.all_to_all(adapter_update, 'store', split_axis=0, concat_axis=0, tile...]
  transfers between devices with their start and end apart: 3 -> 3, of which waited for: 2 -> 2; matrix products, arithmetic and copies ran while one was open for 29% -> 32% of each run, Pallas kernels for 0% -> 0%
where the time goes in v1:
time: 95.5 us; the launch traced here: 94.9 us
  waiting for transfers between devices  19.7 us (21%)
  matrix products  17.5 us (18%)
  blocking collectives  15.2 us (16%)
  between operations  13.7 us (14%)
  starting transfers between devices  10.9 us (11%)
  other arithmetic  10.3 us (11%)
  local copies, waits for them, and re-layouts  7.7 us (8%)
    all_gather x1, blocking collectives, summed_here(): parts = lax.all_gather(array, axis, axis=0, tiled=False)  15.2 us
    all_to_all x1, waiting for transfers between devices, body(): lax.all_to_all(adapter_update, 'store', split_axis=0, concat_axis=0, tile...  12.9 us
    dot_general x1, matrix products, body(): jnp.dot(tokens, joined_weight.reshape(d_model, head_slice * column_list),...  9.86 us
    all_to_all x1, starting transfers between devices, body(): lax.all_to_all(outgoing.reshape(n_store, CAP, width_slice), 'store', spli...  7.12 us
    all_to_all x1, waiting for transfers between devices, body(): lax.all_to_all(outgoing.reshape(n_store, CAP, width_slice), 'store', spli...  6.79 us
    reduce_or x1, other arithmetic, body(): adapter_hot = jnp.any(adapter_hot, axis=1)  4.45 us
    all_to_all x1, starting transfers between devices, body(): lax.all_to_all(adapter_update, 'store', split_axis=0, concat_axis=0, tile...  3.77 us
    dot_general x1, matrix products, body(): jnp.einsum('oxbl,blpj->oxpj', spread_rows, up_weight, preferred_element_t...  2.99 us
  transfers between devices with their start and end apart: 3, of which 2 were waited for; matrix products, arithmetic and copies ran while one was open for 32% of the time, Pallas kernels for 0%

profile of v1, /device:TPU:0, one launch (start us, length us, event | category | flops | bytes accessed | tf_op | source)
XLA Modules:
  0.0 94.9 jit_solution(4126861213734665776)
XLA Ops:
  6.5 1.7 %copy.72 = bf16[32,8,256]{2,0,1:T(8,128)(2,1)} copy(bf16[32,8,256]{2,1,0:T(8,128)(2,1)} %param.17) | data formatting | bytes 262144 | tf_op args[8]
  8.3 1.3 %select_reduce_fusion.1 = s32[2048]{0:T(1024)S(1)} fusion(s32[128]{0:T(128)} %param.14, s32[2048]{0:T(1024)} %param.13), kind=kLoop, calls=%fused_computation.25 | loop fusion | flops 784384 | bytes 16896 | tf_op jit(solution)/shard_map/reduce_sum | solution.py:73
  9.7 0.1 copy.73
  9.8 2.8 %select_reduce_fusion = s32[16,128]{0,1:T(8,128)S(1)} fusion(s32[16,128]{0,1:T(8,128)S(1)} %copy.73), kind=kOutput, calls=%fused_computation.21 | output fusion | flops 4356096 | bytes 16384 | tf_op jit(solution)/shard_map/jit(cumsum)/reduce_window_sum | solution.py:80
  12.7 2.0 %scatter_custom_fusion = bf16[256,1024]{1,0:T(8,128)(2,1)} fusion(s32[128]{0:T(128)S(1)} %fusion.66, bf16[128,8192]{1,0:T(8,128)(2,1)S(1)} %copy-done, s32[]{:T(128)} %constant.35.clone.1, s32[]{:T(128)S(6)} %select_n.75, bf16[]{:T(256)} %constant.73.clone.1), kind=kCustom, calls=%fused_computation.46 | custom fusion | bytes 786442 | tf_op jit(solution)/shard_map/scatter | solution.py:115
  14.6 7.1 %all-to-all-start = ((bf16[16,16,1024]{2,1,0:T(8,128)(2,1)}), bf16[16,16,1024]{2,1,0:T(8,128)(2,1)S(1)}, u32[]{:S(2)}, u32[]{:S(2)}) async-start(bf16[16,16,1024]{2,1,0:T(8,128)(2,1)} %bitcast.10), calls=%async_computation | async-start | bytes 1048576 | tf_op jit(solution)/shard_map/all_to_all | solution.py:116
  21.9 4.4 %and_reduce_fusion = pred[16,16,8]{2,1,0:T(8,128)(4,1)S(1)} fusion(pred[16,128,8]{1,2,0:T(8,128)(4,1)S(1)} %iota_compare_fusion.4, pred[16,128,16]{1,2,0:T(8,128)(4,1)S(1)} %fusion.41), kind=kLoop, calls=%fused_computation.27 | loop fusion | flops 522240 | bytes 51200 | tf_op jit(solution)/shard_map/reduce_or | solution.py:131
  26.3 0.1 copy.75
  26.5 6.8 %all-to-all-done = bf16[16,16,1024]{2,1,0:T(8,128)(2,1)S(1)} async-done(((bf16[16,16,1024]{2,1,0:T(8,128)(2,1)}), bf16[16,16,1024]{2,1,0:T(8,128)(2,1)S(1)}, u32[]{:S(2)}, u32[]{:S(2)}) %all-to-all-start) | async-done | bytes 524320 | tf_op jit(solution)/shard_map/all_to_all | solution.py:116
  33.3 2.0 %fusion.12 = f32[16,16,64]{2,1,0:T(8,128)S(1)} fusion(bf16[8,1024,64]{1,2,0:T(8,128)(2,1)} %param.11, bf16[16,16,1024]{2,1,0:T(8,128)(2,1)S(1)} %all-to-all-done, pred[16,16,8]{1,2,0:T(8,128)(4,1)S(1)} %copy.75), kind=kOutput, calls=%fused_computation.13 | convolution fusion | flops 268681216 | bytes 1640448 | tf_op jit(solution)/shard_map/hbm,gmq->hbgq/dot_general | solution.py:132
  35.3 15.2 %all-gather = f32[128,16,64]{2,1,0:T(8,128)S(1)} all-gather(f32[16,16,64]{2,1,0:T(8,128)S(1)} %fusion.12), channel_id=2, replica_groups=mesh['store'=16,'ctx'=8] {'ctx'}, dimensions={0}, use_global_device_ids=true | all-gather | bytes 589824 | tf_op jit(solution)/shard_map/all_gather | solution.py:15
  50.5 3.0 %fusion.6 = bf16[16,16,1,1280]{3,1,2,0:T(8,128)(2,1)} fusion(bf16[8,64,1,1280]{3,1,2,0:T(8,128)(2,1)} %param.12, pred[16,16,8]{1,2,0:T(8,128)(4,1)S(1)} %copy.75, bf16[16,16,64]{2,1,0:T(8,128)(2,1)S(1)} %reduce_sum.58), kind=kOutput, calls=%fused_computation.7 | convolution fusion | flops 336003072 | bytes 2000896 | tf_op jit(solution)/shard_map/oxbl,blpj->oxpj/dot_general | solution.py:140
  53.5 3.8 %all-to-all-start.1 = ((bf16[16,16,1,1280]{3,1,2,0:T(8,128)(2,1)}), bf16[16,16,1,1280]{3,1,2,0:T(8,128)(2,1)S(1)}, u32[]{:S(2)}, u32[]{:S(2)}) async-start(bf16[16,16,1,1280]{3,1,2,0:T(8,128)(2,1)} %fusion.6), calls=%async_computation.1 | async-start | bytes 1310720 | tf_op jit(solution)/shard_map/all_to_all | solution.py:143
  57.4 0.1 add.100
  57.4 0.1 select_reduce_fusion.2
  57.5 0.1 fusion.42
  57.7 0.3 multiply_cosine_fusion.1
  58.0 12.9 %all-to-all-done.1 = bf16[16,16,1,1280]{3,1,2,0:T(8,128)(2,1)S(1)} async-done(((bf16[16,16,1,1280]{3,1,2,0:T(8,128)(2,1)}), bf16[16,16,1,1280]{3,1,2,0:T(8,128)(2,1)S(1)}, u32[]{:S(2)}, u32[]{:S(2)}) %all-to-all-start.1) | async-done | bytes 655392 | tf_op jit(solution)/shard_map/all_to_all | solution.py:143
  70.9 1.6 %gather_fusion = bf16[128,1280]{1,0:T(8,128)(2,1)} fusion(bf16[256,1280]{1,0:T(8,128)(2,1)S(1)} %bitcast.145, s32[1024]{0:T(1024)S(1)} %pad_clamp_fusion), kind=kCustom, calls=%fused_computation | custom fusion | bytes 655872 | tf_op jit(solution)/shard_map/gather | solution.py:144
  72.5 9.9 %fusion.7 = f32[128,1,1280]{2,0,1:T(8,128)S(1)} fusion(bf16[128,8192]{1,0:T(8,128)(2,1)S(1)} %copy-done, bf16[8192,1,1280]{2,0,1:T(8,128)(2,1)} %param.10, bf16[128,1280]{1,0:T(8,128)(2,1)} %gather_fusion), kind=kOutput, calls=%fused_computation.8 | convolution fusion | flops 2684846080 | bytes 24051712 | tf_op jit(solution)/shard_map/dot_general | solution.py:145
  82.5 0.1 copy.94
  82.6 0.7 copy.82
  83.3 0.3 fusion.56
  83.6 0.1 maximum_bitcast_fusion
  83.7 0.2 fusion.69
  83.9 0.2 fusion.31
  84.1 0.1 pad_maximum_fusion
  84.3 0.3 fusion.38
  84.6 1.2 %fusion.70 = (f32[128,8]{0,1:T(8,128)S(1)}, f32[128,1,8,256]{0,3,2,1:T(8,128)S(1)}) fusion(bf16[128,8,128]{2,0,1:T(8,128)(2,1)S(1)} %pad_maximum_fusion, bf16[256,8,256]{2,0,1:T(8,128)(2,1)} %all-gather.3.cloned.1.call-done, s32[]{:T(128)S(6)} %select_n.68, pred[128,256]{0,1:T(8,128)(4,1)S(1)} %fusion.42), kind=kOutput, calls=%fused_computation.112 | convolution fusion | flops 67894272 | bytes 1413124 | tf_op jit(solution)/shard_map/rhgd,thd->rhgt/dot_general | solution.py:48
  85.8 0.2 fusion.20
  86.1 1.2 %fusion.16 = bf16[128,1,8,128]{0,3,2,1:T(8,128)(2,1)S(1)} fusion(f32[128,1,8,256]{0,3,2,1:T(8,128)S(1)} %get-tuple-element.18, f32[128,8]{0,1:T(8,128)S(1)} %fusion.60, pred[128,256]{0,1:T(8,128)(4,1)S(1)} %fusion.42, f32[128,8]{0,1:T(8,128)S(1)} %get-tuple-element.12, f32[128,128]{0,1:T(8,128)S(1)} %copy-done.1, f32[128,8]{0,1:T(8,128)S(1)} %get-tuple-element.11, ...), kind=kOutput, calls=%fused_computation.18 | convolution fusion | flops 68419584 | bytes 1486856 | tf_op jit(solution)/shard_map/rhgt,thd->rhgd/dot_general | solution.py:61
  87.2 0.9 copy.83
  (30 shorter events, 0.4 us)
Async XLA Ops:
  6.5 6.1 %copy-start = (bf16[128,8192]{1,0:T(8,128)(2,1)S(1)}, bf16[128,8192]{1,0:T(8,128)(2,1)}, u32[]{:S(2)}) copy-start(bf16[128,8192]{1,0:T(8,128)(2,1)} %param.9) | copy-start | bytes 6291460
  6.5 19.9 %copy-start.2 = (s32[128,8]{0,1:T(8,128)S(1)}, s32[128,8]{0,1:T(8,128)}, u32[]{:S(2)}) copy-start(s32[128,8]{0,1:T(8,128)} %param.15) | copy-start | bytes 12292
  6.5 78.1 %all-gather.3.cloned.1.call-start = ((), (), s32[]{:S(2)}) async-start(), calls=%async_computation.2 | async-start | bytes 1179648 | tf_op jit(solution)/shard_map/all_gather | solution.py:106
  14.6 18.6 %all-to-all-start = ((bf16[16,16,1024]{2,1,0:T(8,128)(2,1)}), bf16[16,16,1024]{2,1,0:T(8,128)(2,1)S(1)}, u32[]{:S(2)}, u32[]{:S(2)}) async-start(bf16[16,16,1024]{2,1,0:T(8,128)(2,1)} %bitcast.10), calls=%async_computation | async-start | bytes 1048576 | tf_op jit(solution)/shard_map/all_to_all | solution.py:116
  50.5 6.8 %copy-start.3 = (s32[128]{0:T(128)S(1)}, s32[128]{0:T(128)}, u32[]{:S(2)}) copy-start(s32[128]{0:T(128)} %param.16) | copy-start | bytes 1540
  53.5 17.4 %all-to-all-start.1 = ((bf16[16,16,1,1280]{3,1,2,0:T(8,128)(2,1)}), bf16[16,16,1,1280]{3,1,2,0:T(8,128)(2,1)S(1)}, u32[]{:S(2)}, u32[]{:S(2)}) async-start(bf16[16,16,1,1280]{3,1,2,0:T(8,128)(2,1)} %fusion.6), calls=%async_computation.1 | async-start | bytes 1310720 | tf_op jit(solution)/shard_map/all_to_all | solution.py:143
  84.1 1.9 %copy-start.1 = (f32[128,128]{0,1:T(8,128)S(1)}, f32[128,128]{0,1:T(8,128)}, u32[]{:S(2)}) copy-start(f32[128,128]{0,1:T(8,128)} %copy.82) | copy-start | bytes 196612
Sparse Core Ops, SparseCore 0:
  9.1 26.0 all-gather.2
